TPU v7x, 128 devices: a whole 4x4x4 slice. The times are simulated.
128 devices in a mesh: gx: 16 (over y, z), gy: 8 (over x, core).
Axes of the slice: x: 4, y: 4, z: 4, core: 2. Of those that a mesh axis runs over, the one named last changes fastest.
Arguments:
- features: bfloat16 [2048, 512, 128], P('gx', 'gy'), may hold values from -6 to 6
- cotangent: bfloat16 [2048, 512, 128], P('gx', 'gy'), may hold values from -31 to 31
- kernel: float32 [7, 7, 128], replicated, may hold values from -0.875 to 0.875
- kernel_bias: float32 [128], replicated, may hold values from -3 to 3
- norm_gain: float32 [128], replicated, may hold values from 0.1 to 1.9
- norm_shift: float32 [128], replicated, may hold values from -3 to 3
- w_up: bfloat16 [128, 512], replicated, may hold values from -0.5 to 0.5
- b_up: float32 [512], replicated, may hold values from -3 to 3
- w_down: bfloat16 [512, 128], replicated, may hold values from -0.25 to 0.25
- b_down: float32 [128], replicated, may hold values from -3 to 3
- layer_scale: float32 [128], replicated, may hold values from 0.3 to 3
Outputs:
- d_features: bfloat16 [2048, 512, 128], P('gx', 'gy')
- d_kernel: float32 [7, 7, 128], replicated
- d_kernel_bias: float32 [128], replicated
- d_norm_gain: float32 [128], replicated
- d_norm_shift: float32 [128], replicated
- d_w_up: float32 [128, 512], replicated
- d_b_up: float32 [512], replicated
- d_w_down: float32 [512, 128], replicated
- d_b_down: float32 [128], replicated
- d_layer_scale: float32 [128], replicated
All inputs are finite; a program needn't handle non-finite values.
Results may differ from a plain program's by a relative error of at most 0.0072.
Values may be sent and summed in bfloat16 or wider, within the bound.
No kernel may reach another device: no remote copies, remote signals or barrier semaphores. Data moves between devices by JAX's collectives and lax.ppermute only.
A program may use at most 64 MiB of HBM per device.

v0:
```python
import math
import jax
import jax.numpy as jnp
from jax import lax
from jax.sharding import PartitionSpec as P

EPSILON = 1e-06


def extended(cells, sides, width):
    for axis, dim in sides:
        count = lax.axis_size(axis)
        head = lax.slice_in_dim(cells, 0, width, axis=dim)
        tail = lax.slice_in_dim(cells, cells.shape[dim] - width, cells.shape[dim], axis=dim)
        cells = jnp.concatenate(
            [
                lax.ppermute(tail, axis, [(i, (i + 1) % count) for i in range(count)]),
                cells,
                lax.ppermute(head, axis, [((i + 1) % count, i) for i in range(count)]),
            ],
            axis=dim,
        )
    return cells


def gelu_pair(hidden):
    erf_part = jax.scipy.special.erf(hidden * 0.7071067811865476)
    value = 0.5 * hidden * (1.0 + erf_part)
    slope_value = (
        0.5 * (1.0 + erf_part) + hidden * jnp.exp(-0.5 * hidden * hidden) * 0.3989422804014327
    )
    return (value, slope_value)


def product(spec, left, right):
    return jnp.einsum(spec, left, right, preferred_element_type=jnp.float32)


def depthwise(padded, kernel, row_count, col_count):
    tap_count = kernel.shape[0]
    accum = jnp.zeros((row_count, col_count, kernel.shape[2]), jnp.float32)
    for row_tap in range(tap_count):
        for col_tap in range(tap_count):
            window = padded[row_tap : row_tap + row_count, col_tap : col_tap + col_count]
            accum = accum + window.astype(jnp.float32) * kernel[row_tap, col_tap]
    return accum


def spread_back(padded, kernel, row_count, col_count):
    tap_count = kernel.shape[0]
    edge_cells = tap_count - 1
    accum = jnp.zeros((row_count, col_count, kernel.shape[2]), jnp.float32)
    for row_tap in range(tap_count):
        for col_tap in range(tap_count):
            window = padded[
                edge_cells - row_tap : edge_cells - row_tap + row_count,
                edge_cells - col_tap : edge_cells - col_tap + col_count,
            ]
            accum = accum + window * kernel[row_tap, col_tap]
    return accum


def kernel_grad(slopes_in, padded, tap_count):
    row_count, col_count = (slopes_in.shape[0], slopes_in.shape[1])
    rows_out = []
    for row_tap in range(tap_count):
        line = []
        for col_tap in range(tap_count):
            window = padded[row_tap : row_tap + row_count, col_tap : col_tap + col_count].astype(
                jnp.float32
            )
            line.append(jnp.sum(slopes_in * window, axis=(0, 1)))
        rows_out.append(jnp.stack(line, 0))
    return jnp.stack(rows_out, 0)


def mask_edges(padded, width):
    col_total = padded.shape[1]
    inner_cols = col_total - 2 * width
    grid_cols = inner_cols * lax.axis_size("gy")
    col_place = lax.axis_index("gy") * inner_cols + lax.iota(jnp.int32, col_total) - width
    keep_mask = (col_place >= 0) & (col_place < grid_cols)
    return jnp.where(keep_mask[None, :, None], padded, jnp.zeros((), padded.dtype))


def layer_back(conv_out, cotan, norm_gain, norm_shift, w_up, b_up, w_down, b_down, layer_scale):
    chan_mean = jnp.mean(conv_out, axis=-1, keepdims=True)
    centred = conv_out - chan_mean
    inv_std = lax.rsqrt(jnp.mean(centred * centred, axis=-1, keepdims=True) + EPSILON)
    normed = centred * inv_std
    normal_out = (normed * norm_gain + norm_shift).astype(jnp.bfloat16)
    hidden = product("rwc,ce->rwe", normal_out, w_up) + b_up
    active, gelu_slope = gelu_pair(hidden)
    active = active.astype(jnp.bfloat16)
    output = product("rwe,ec->rwc", active, w_down) + b_down
    cot_float = cotan.astype(jnp.float32)
    d_output = (cot_float * layer_scale).astype(jnp.bfloat16)
    d_active = product("rwc,ec->rwe", d_output, w_down)
    d_hidden = (d_active * gelu_slope).astype(jnp.bfloat16)
    d_normal = product("rwe,ce->rwc", d_hidden, w_up)
    d_normed = d_normal * norm_gain
    first_mean = jnp.mean(d_normed, axis=-1, keepdims=True)
    second_mean = jnp.mean(d_normed * normed, axis=-1, keepdims=True)
    d_conv = inv_std * (d_normed - first_mean - normed * second_mean)
    d_gain = jnp.sum(d_normal * normed, axis=(0, 1))
    d_shift = jnp.sum(d_normal, axis=(0, 1))
    d_wup = product("rwc,rwe->ce", normal_out, d_hidden)
    d_bup = jnp.sum(d_hidden.astype(jnp.float32), axis=(0, 1))
    d_wdown = product("rwe,rwc->ec", active, d_output)
    d_bdown = jnp.sum(d_output.astype(jnp.float32), axis=(0, 1))
    d_lscale = jnp.sum(cot_float * output, axis=(0, 1))
    return (d_conv, (d_gain, d_shift, d_wup, d_bup, d_wdown, d_bdown, d_lscale))


def local(
    features,
    cotangent,
    kernel,
    kernel_bias,
    norm_gain,
    norm_shift,
    w_up,
    b_up,
    w_down,
    b_down,
    layer_scale,
):
    tap_count = kernel.shape[0]
    reach_cells = tap_count // 2
    row_count, col_count = (features.shape[0], features.shape[1])
    padded_x = mask_edges(extended(features, (("gx", 0), ("gy", 1)), reach_cells), reach_cells)
    conv_out = depthwise(padded_x, kernel, row_count, col_count) + kernel_bias
    d_conv, layer_grads = layer_back(
        conv_out, cotangent, norm_gain, norm_shift, w_up, b_up, w_down, b_down, layer_scale
    )
    d_kern = kernel_grad(d_conv, padded_x, tap_count)
    d_kbias = jnp.sum(d_conv, axis=(0, 1))
    padded_slope = mask_edges(extended(d_conv, (("gx", 0), ("gy", 1)), reach_cells), reach_cells)
    spread = spread_back(padded_slope, kernel, row_count, col_count)
    d_features = (cotangent.astype(jnp.float32) + spread).astype(jnp.bfloat16)
    d_gain, d_shift, d_wup, d_bup, d_wdown, d_bdown, d_lscale = layer_grads
    summed = lax.psum(
        (d_kern, d_kbias, d_gain, d_shift, d_wup, d_bup, d_wdown, d_bdown, d_lscale), ("gx", "gy")
    )
    factor = 1.0 / math.sqrt(row_count * col_count * lax.axis_size("gx") * lax.axis_size("gy"))
    return (d_features,) + tuple((entry * factor for entry in summed))


def solution(mesh):
    placed = (P("gx", "gy", None), P("gx", "gy", None), P(), P(), P(), P(), P(), P(), P(), P(), P())
    return jax.shard_map(
        local,
        mesh=mesh,
        in_specs=placed,
        out_specs=(P("gx", "gy", None), P(), P(), P(), P(), P(), P(), P(), P(), P()),
        check_vma=False,
    )
```

profile of v0, /device:TPU:1, one launch (start us, length us, event | category | flops | bytes accessed | tf_op | source)
XLA Modules:
  0.0 487.0 jit_solution(8291468814353680774)
XLA Ops:
  7.2 0.0 copy-start
  7.2 0.0 copy-start.6
  7.2 0.0 all-reduce.4.cloned.1.call-start
  7.3 0.0 copy-start.3
  7.3 3.1 copy.22
  10.4 0.1 fusion.166
  10.4 2.5 collective-permute-start
  13.0 4.9 %collective-permute-start.1 = (bf16[3,64,128]{2,0,1:T(4,128)(2,1)S(1)}, bf16[3,64,128]{2,0,1:T(4,128)(2,1)S(1)}, u32[]{:S(2)}, u32[]{:S(2)}) collective-permute-start(bf16[3,64,128]{2,0,1:T(4,128)(2,1)S(1)} %get-tuple-element.93), channel_id=1, source_target_pairs={{8,0},{16,8},{24,16},{32,24},{40,32},{48,40},{56,48},{64,56},{72,6... | collective-permute-start | bytes 147464 | tf_op jit(solution)/shard_map/ppermute | solution.py:19
  17.9 0.0 copy-done.6
  18.0 1.1 convert_reduce_fusion.1
  19.1 0.1 collective-permute-done
  19.2 0.1 collective-permute-done.1
  19.2 0.1 pad_maximum_fusion.5
  19.3 2.6 collective-permute-start.2
  21.9 0.0 collective-permute-start.3
  21.9 1.7 collective-permute-done.2
  23.6 2.4 collective-permute-done.3
  26.0 2.9 maximum_select_fusion.1
  29.0 33.0 %fusion.163 = (f32[128,64]{0,1:T(8,128)S(1)}, f32[128,64,128]{2,0,1:T(8,128)S(1)}) fusion(f32[128]{0:T(128)S(1)} %copy-done.11, f32[128]{0:T(128)S(1)} %get-tuple-element.141, bf16[134,70,128]{2,0,1:T(8,128)(2,1)S(1)} %maximum_select_fusion.1, f32[128]{0:T(128)S(1)} %get-tuple-element.142, f32[128]{0:T(128)S(1)} %get-tuple-element.95, ...), kind=kLoop, calls=%fused_computation.403 | loop fusion | flops 155181056 | bytes 107013120 | tf_op jit(solution)/shard_map/reduce_sum | solution.py:87
  62.0 0.0 copy-start.7
  62.0 0.0 copy-start.8
  62.0 0.0 copy-start.9
  62.0 2.7 multiply_reduce_fusion.2
  64.8 0.0 copy-start.4
  64.8 0.0 copy-start.12
  64.8 8.6 %multiply_convert_fusion = (bf16[128,64,512]{2,0,1:T(8,128)(2,1)}, f32[128,64,512]{2,0,1:T(8,128)S(1)}) fusion(f32[512]{0:T(512)S(1)} %copy-done.9, bf16[128,512]{1,0:T(8,128)(2,1)S(1)} %copy-done, f32[128,64,128]{2,0,1:T(8,128)S(1)} %get-tuple-element.85, f32[128]{0:T(128)S(1)} %copy-done.8, f32[128]{0:T(128)S(1)} %copy-done.7, ...), kind=kOutput, calls=%fused_computation.7 | convolution fusion | flops 1104150528 | bytes 29559808 | tf_op jit(solution)/shard_map/rwc,ce->rwe/dot_general | solution.py:36
  73.5 10.9 %convert_reduce_fusion = (f32[512]{0:T(512)S(1)}, bf16[128,64,512]{2,0,1:T(8,128)(2,1)S(1)}) fusion(f32[128,64,512]{2,0,1:T(8,128)S(1)} %get-tuple-element.147, f32[512]{0:T(512)S(1)} %copy-done.9, bf16[512,128]{1,0:T(8,128)(2,1)S(1)} %copy-done.12, f32[128]{0:T(128)S(1)} %copy-done.10, bf16[128,64,128]{2,1,0:T(8,128)(2,1)S(1)} %copy-done.4), kind=kOutput, calls=%fused_computation.8 | convolution fusion | flops 1131412992 | bytes 27398656 | tf_op jit(solution)/shard_map/rwc,ec->rwe/dot_general | solution.py:36
  84.4 4.2 convolution_bitcast_fusion.1
  88.6 4.8 multiply_reduce_fusion
  93.3 0.0 slice-start
  93.3 13.4 %fusion.102 = (f32[128]{0:T(128)S(1)}, f32[128]{0:T(128)S(1)}, f32[128]{0:T(128)S(1)}, f32[128]{0:T(128)S(1)}, f32[128]{0:T(128)S(1)}, /*index=5*/f32[128]{0:T(1...) fusion(bf16[134,70,128]{2,0,1:T(8,128)(2,1)S(1)} %maximum_selec, ...), kind=kLoop, calls=%fused_computation.208 | loop fusion | flops 63960832 | bytes 50472448 | tf_op jit(solution)/shard_map/reduce_sum | solution.py:72
  106.7 0.0 copy-start.2
  106.8 0.0 slice-start.1
  106.8 11.0 %fusion.84 = (f32[128]{0:T(128)S(1)}, f32[128]{0:T(128)S(1)}, f32[128]{0:T(128)S(1)}, f32[128]{0:T(128)S(1)}, f32[128]{0:T(128)S(1)}, /*index=5*/f32[128]{0:T(12...) fusion(f32[128,64,128]{2,0,1:T(8,128)S(1)} %get-tuple-element.8, ...), kind=kLoop, calls=%fused_computation.190 | loop fusion | flops 56620800 | bytes 41952256 | tf_op jit(solution)/shard_map/reduce_sum | solution.py:72
  117.8 0.0 copy-start.5
  117.8 8.2 %fusion.43 = (f32[128]{0:T(128)S(1)}, f32[128]{0:T(128)S(1)}, f32[128]{0:T(128)S(1)}, f32[128]{0:T(128)S(1)}, f32[128]{0:T(128)S(1)}, /*index=5*/f32[128]{0:T(12...) fusion(f32[128,64,128]{2,0,1:T(8,128)S(1)} %get-tuple-element.8, ...), kind=kLoop, calls=%fused_computation.149 | loop fusion | flops 41941248 | bytes 31464448 | tf_op jit(solution)/shard_map/reduce_sum | solution.py:72
  126.2 0.0 copy-start.13
  126.2 4.3 convolution_bitcast_fusion
  130.5 0.0 copy-done.13
  130.5 6.2 %fusion.105 = f32[128]{0:T(128)S(1)} fusion(bf16[128,64,512]{2,0,1:T(8,128)(2,1)} %get-tuple-element.146, f32[128]{0:T(128)S(1)} %copy-done.13, bf16[128,64,128]{2,1,0:T(8,128)(2,1)S(1)} %copy-done.5, bf16[512,128]{1,0:T(8,128)(2,1)S(1)} %copy-done.12), kind=kOutput, calls=%fused_computation.211 | convolution fusion | flops 1077936000 | bytes 10617856 | tf_op jit(solution)/shard_map/rwe,ec->rwc/dot_general | solution.py:36
  137.0 67.9 %all-reduce = (f32[7,7,128]{2,1,0:T(8,128)S(1)}, f32[128]{0:T(128)S(1)}, f32[128]{0:T(128)S(1)}, f32[128]{0:T(128)S(1)}, f32[512]{0:T(512)S(1)}, /*index=5*/f32[128]{0:T(128)S(1)}, f32[128]{0:T(128)S(1)}) all-reduce(f32[7,7,128]{2,1,0:T(8,128)S(1)} %constant_dynamic-update-slice_fusion, ...), channel_id=1, replica_groups=mesh['gx'=16,'gy'=8] {'gx','gy'}, use_global_device_ids=true, to_apply=%region_53.54 | all-reduce | flops 7424 | bytes 59392 | tf_op jit(solution)/shard_map/psum | solution.py:142
  204.9 0.6 broadcast_multiply_fusion.5
  205.6 0.6 broadcast_multiply_fusion.6
  206.1 0.5 broadcast_multiply_fusion.10
  206.6 0.5 broadcast_multiply_fusion.11
  207.2 0.5 broadcast_multiply_fusion.7
  207.7 0.5 broadcast_multiply_fusion.8
  208.2 0.0 collective-permute-start.4
  208.2 4.8 collective-permute-start.5
  213.0 0.0 all-reduce.4.cloned.1.call-update
  213.0 0.5 broadcast_multiply_fusion.9
  213.5 1.8 collective-permute-done.4
  215.3 0.0 collective-permute-done.5
  215.3 1.1 pad_maximum_fusion.2
  216.4 1.5 collective-permute-start.6
  217.9 0.8 collective-permute-start.7
  218.8 136.7 %all-reduce.4.cloned.1.call-done = (f32[128,512]{1,0:T(8,128)}, f32[512,128]{1,0:T(8,128)}) async-done(((f32[128,512]{1,0:T(8,128)}, f32[512,128]{1,0:T(8,128)}), (f32[128,512]{1,0:T(8,128)}, f32[512,128]{1,0:T(8,128)})) %all-reduce.4.cloned.1.call-update) | async-done | bytes 524304 | tf_op jit(solution)/shard_map/psum | solution.py:142
  355.4 1.7 broadcast_multiply_fusion
  357.1 1.7 broadcast_multiply_fusion.1
  358.8 0.0 collective-permute-done.6
  358.8 0.0 collective-permute-done.7
  358.8 5.5 %maximum_select_fusion = f32[134,70,128]{2,0,1:T(8,128)} fusion(f32[134,3,128]{2,0,1:T(8,128)S(1)} %collective-permute-done.7, f32[3,64,128]{2,0,1:T(4,128)S(1)} %collective-permute-done.5, f32[128,64,128]{2,0,1:T(8,128)} %copy-done.2, f32[3,64,128]{2,0,1:T(4,128)S(1)} %collective-permute-done.4, f32[134,3,128]{2,0,1:T(8,128)S(1)} %collective-permute-done.6, ...), kind=kLoop, calls=%fused_computation.111 | loop fusion | flops 6003200 | bytes 9605190 | tf_op jit(solution)/shard_map/jit(_where)/select_n | solution.py:83
  364.3 111.4 %fusion.104 = bf16[128,64,128]{2,0,1:T(8,128)(2,1)} fusion(f32[134,70,128]{2,0,1:T(8,128)} %maximum_select_fusion, f32[128]{0:T(128)S(1)} %get-tuple-element.141, f32[128]{0:T(128)S(1)} %get-tuple-element.142, f32[128]{0:T(128)S(1)} %get-tuple-element.95, f32[128]{0:T(128)S(1)} %get-tuple-element.96, f32[128]{0:T(128)S(1)} %get-tuple-element.97, ...), kind=kLoop, calls=%fused_computation.210 | loop fusion | flops 104857600 | bytes 209740288 | tf_op jit(solution)/shard_map/convert_element_type | solution.py:140
  475.7 4.3 copy.27
  (40 shorter events, 0.4 us)
Async XLA Ops:
  7.2 57.6 %copy-start = (bf16[128,512]{1,0:T(8,128)(2,1)S(1)}, bf16[128,512]{1,0:T(8,128)(2,1)}, u32[]{:S(2)}) copy-start(bf16[128,512]{1,0:T(8,128)(2,1)} %param.17) | copy-start | bytes 393220
  7.2 10.7 %copy-start.6 = (f32[7,7,128]{2,1,0:T(8,128)S(1)}, f32[7,7,128]{2,1,0:T(8,128)}, u32[]{:S(2)}) copy-start(f32[7,7,128]{2,1,0:T(8,128)} %param.13) | copy-start | bytes 75268
  7.2 10.7 %copy-start.10 = (f32[128]{0:T(128)S(1)}, f32[128]{0:T(128)}, u32[]{:S(2)}) copy-start(f32[128]{0:T(128)} %param.21) | copy-start | bytes 1540
  7.2 348.2 %all-reduce.4.cloned.1.call-start = ((), (), s32[]{:S(2)}) async-start(), calls=%async_computation | async-start | bytes 1048576 | tf_op jit(solution)/shard_map/psum | solution.py:142
  7.3 10.7 %copy-start.3 = (bf16[128,64,128]{2,1,0:T(8,128)(2,1)S(1)}, bf16[128,64,128]{2,1,0:T(8,128)(2,1)}, u32[]{:S(2)}) copy-start(bf16[128,64,128]{2,1,0:T(8,128)(2,1)} %param.12) | copy-start | bytes 6291460
  10.4 8.8 %collective-permute-start = (bf16[3,64,128]{2,0,1:T(4,128)(2,1)S(1)}, bf16[3,64,128]{2,0,1:T(4,128)(2,1)S(1)}, u32[]{:S(2)}, u32[]{:S(2)}) collective-permute-start(bf16[3,64,128]{2,0,1:T(4,128)(2,1)S(1)} %get-tuple-element.92), channel_id=1, source_target_pairs={{0,8},{8,16},{16,24},{24,32},{32,40},{40,48},{48,56},{56,64},{64,7... | collective-permute-start | bytes 147464 | tf_op jit(solution)/shard_map/ppermute | solution.py:17
  13.0 6.3 %collective-permute-start.1 = (bf16[3,64,128]{2,0,1:T(4,128)(2,1)S(1)}, bf16[3,64,128]{2,0,1:T(4,128)(2,1)S(1)}, u32[]{:S(2)}, u32[]{:S(2)}) collective-permute-start(bf16[3,64,128]{2,0,1:T(4,128)(2,1)S(1)} %get-tuple-element.93), channel_id=1, source_target_pairs={{8,0},{16,8},{24,16},{32,24},{40,32},{48,40},{56,48},{64,56},{72,6... | collective-permute-start | bytes 147464 | tf_op jit(solution)/shard_map/ppermute | solution.py:19
  19.1 9.9 %copy-start.11 = (f32[128]{0:T(128)S(1)}, f32[128]{0:T(128)}, u32[]{:S(2)}) copy-start(f32[128]{0:T(128)} %param.14) | copy-start | bytes 1540
  19.3 4.3 collective-permute-start.2
  21.9 4.1 collective-permute-start.3
  62.0 2.8 copy-start.7
  62.0 2.8 copy-start.8
  62.0 2.8 copy-start.9
  64.8 8.7 %copy-start.4 = (bf16[128,64,128]{2,1,0:T(8,128)(2,1)S(1)}, bf16[128,64,128]{2,1,0:T(8,128)(2,1)}, u32[]{:S(2)}) copy-start(bf16[128,64,128]{2,1,0:T(8,128)(2,1)} %param.12) | copy-start | bytes 6291460
  64.8 8.6 %copy-start.12 = (bf16[512,128]{1,0:T(8,128)(2,1)S(1)}, bf16[512,128]{1,0:T(8,128)(2,1)}, u32[]{:S(2)}) copy-start(bf16[512,128]{1,0:T(8,128)(2,1)} %param.19) | copy-start | bytes 393220
  93.3 32.8 %slice-start = ((s8[8388608]{0:T(1024)(128)(4,1)}), s8[4194304]{0:T(1024)(128)(4,1)S(1)}, s32[]{:S(2)}) async-start(s8[8388608]{0:T(1024)(128)(4,1)} %bitcast.185), calls=%async_computation.1 | async-start | bytes 8388608
  106.7 19.3 %copy-start.2 = (f32[128,64,128]{2,0,1:T(8,128)}, f32[128,64,128]{2,0,1:T(8,128)S(1)}, u32[]{:S(2)}) copy-start(f32[128,64,128]{2,0,1:T(8,128)S(1)} %get-tuple-element.83) | copy-start | bytes 12582916
  106.8 19.4 %slice-start.1 = ((s8[8388608]{0:T(1024)(128)(4,1)}), s8[4194304]{0:T(1024)(128)(4,1)S(1)}, s32[]{:S(2)}) async-start(s8[8388608]{0:T(1024)(128)(4,1)} %bitcast.185), calls=%async_computation.2 | async-start | bytes 8388608
  117.8 8.3 %copy-start.5 = (bf16[128,64,128]{2,1,0:T(8,128)(2,1)S(1)}, bf16[128,64,128]{2,1,0:T(8,128)(2,1)}, u32[]{:S(2)}) copy-start(bf16[128,64,128]{2,1,0:T(8,128)(2,1)} %param.12) | copy-start | bytes 6291460
  126.2 4.4 copy-start.13
  208.2 7.1 %collective-permute-start.4 = (f32[3,64,128]{2,0,1:T(4,128)S(1)}, f32[3,64,128]{2,0,1:T(4,128)S(1)}, u32[]{:S(2)}, u32[]{:S(2)}) collective-permute-start(f32[3,64,128]{2,0,1:T(4,128)S(1)} %get-tuple-element.88), channel_id=1, source_target_pairs={{0,8},{8,16},{16,24},{24,32},{32,40},{40,48},{48,56},{56,64},{64,7... | collective-permute-start | bytes 294920 | tf_op jit(solution)/shard_map/ppermute | solution.py:17
  208.2 7.1 %collective-permute-start.5 = (f32[3,64,128]{2,0,1:T(4,128)S(1)}, f32[3,64,128]{2,0,1:T(4,128)S(1)}, u32[]{:S(2)}, u32[]{:S(2)}) collective-permute-start(f32[3,64,128]{2,0,1:T(4,128)S(1)} %get-tuple-element.89), channel_id=1, source_target_pairs={{8,0},{16,8},{24,16},{32,24},{40,32},{48,40},{56,48},{64,56},{72,6... | collective-permute-start | bytes 294920 | tf_op jit(solution)/shard_map/ppermute | solution.py:19
  216.4 142.4 %collective-permute-start.6 = (f32[134,3,128]{2,0,1:T(8,128)S(1)}, f32[134,3,128]{2,0,1:T(8,128)S(1)}, u32[]{:S(2)}, u32[]{:S(2)}) collective-permute-start(f32[134,3,128]{2,0,1:T(8,128)S(1)} %get-tuple-element.86), channel_id=1, source_target_pairs={{0,1},{1,2},{2,3},{3,4},{4,5},{5,6},{6,7},{7,0},{8,9},{9,10},{10,1... | collective-permute-start | bytes 617480 | tf_op jit(solution)/shard_map/ppermute | solution.py:17
  217.9 140.9 %collective-permute-start.7 = (f32[134,3,128]{2,0,1:T(8,128)S(1)}, f32[134,3,128]{2,0,1:T(8,128)S(1)}, u32[]{:S(2)}, u32[]{:S(2)}) collective-permute-start(f32[134,3,128]{2,0,1:T(8,128)S(1)} %get-tuple-element.87), channel_id=1, source_target_pairs={{1,0},{2,1},{3,2},{4,3},{5,4},{6,5},{7,6},{0,7},{9,8},{10,9},{11,1... | collective-permute-start | bytes 617480 | tf_op jit(solution)/shard_map/ppermute | solution.py:19
  364.3 115.7 %copy-start.1 = (bf16[128,512]{1,0:T(8,128)(2,1)S(1)}, bf16[128,512]{1,0:T(8,128)(2,1)}, u32[]{:S(2)}) copy-start(bf16[128,512]{1,0:T(8,128)(2,1)} %param.17) | copy-start | bytes 393220
Sparse Core Ops, SparseCore 0:
  213.1 142.2 all-reduce.3
where the time goes:
time: 490 us; the launch traced here: 487 us
  other arithmetic  198 us (40%)
  waiting for transfers between devices  143 us (29%)
  blocking collectives  67.9 us (14%)
  matrix products  39 us (8%)
  starting transfers between devices  17.3 us (4%)
  between operations  14.7 us (3%)
  local copies, waits for them, and re-layouts  7.79 us (2%)
    psum x1, waiting for transfers between devices, local(): lax.psum((d_kern, d_kbias, d_gain, d_shift, d_wup, d_bup, d_wdown, d_bdow...  137 us
    convert_element_type x1, other arithmetic, local(): d_features = (cotangent.astype(jnp.float32) + spread).astype(jnp.bfloat16)  111 us
    psum x1, blocking collectives, local(): lax.psum((d_kern, d_kbias, d_gain, d_shift, d_wup, d_bup, d_wdown, d_bdow...  67.9 us
    dot_general x6, matrix products, product(): return jnp.einsum(spec, left, right, preferred_element_type=jnp.float32)  39 us
    reduce_sum x1, other arithmetic, layer_back(): chan_mean = jnp.mean(conv_out, axis=-1, keepdims=True)  33 us
    reduce_sum x3, other arithmetic, kernel_grad(): line.append(jnp.sum(slopes_in * window, axis=(0, 1)))  32.6 us
    ppermute x4, starting transfers between devices, extended(): lax.ppermute(head, axis, [((i + 1) % count, i) for i in range(count)])  10.6 us
  transfers between devices with their start and end apart: 9, of which 5 were waited for; matrix products, arithmetic and copies ran while one was open for 1% of the time, Pallas kernels for 0%

commit v1 on v0

--- a/solution.py
+++ b/solution.py
@@ -140,7 +140,10 @@
     d_features = (cotangent.astype(jnp.float32) + spread).astype(jnp.bfloat16)
     d_gain, d_shift, d_wup, d_bup, d_wdown, d_bdown, d_lscale = layer_grads
     summed = lax.psum(
-        (d_kern, d_kbias, d_gain, d_shift, d_wup, d_bup, d_wdown, d_bdown, d_lscale), ("gx", "gy")
+        lax.psum(
+            (d_kern, d_kbias, d_gain, d_shift, d_wup, d_bup, d_wdown, d_bdown, d_lscale), "gy"
+        ),
+        "gx",
     )
     factor = 1.0 / math.sqrt(row_count * col_count * lax.axis_size("gx") * lax.axis_size("gy"))
     return (d_features,) + tuple((entry * factor for entry in summed))

time: 490 us -> 435 us (0.89)
  waiting for transfers between devices: 143 us -> 53.9 us
  blocking collectives: 67.9 us -> 84.7 us
  starting transfers between devices: 17.3 us -> 33.5 us
    psum x1, waiting for transfers between devices: 137 us -> 47.8 us  [local(): lax.psum((d_kern, d_kbias, d_gain, d_shift, d_wup, d_bup, d_wdown, d_bdow...]
    psum x0 -> x1, blocking collectives: none -> 61.3 us  [local(): lax.psum(lax.psum((d_kern, d_kbias, d_gain, d_shift, d_wup, d_bup, d_wdow...]
    psum x1, blocking collectives: 67.9 us -> 23.4 us  [local(): lax.psum((d_kern, d_kbias, d_gain, d_shift, d_wup, d_bup, d_wdown, d_bdow...]
    ppermute x4, starting transfers between devices: 6.71 us -> 21.8 us  [extended(): lax.ppermute(tail, axis, [(i, (i + 1) % count) for i in range(count)])]
  transfers between devices with their start and end apart: 9 -> 10, of which waited for: 5 -> 5; matrix products, arithmetic and copies ran while one was open for 1% -> 29% of each run, Pallas kernels for 0% -> 0%
where the time goes in v1:
time: 435 us; the launch traced here: 431 us
  other arithmetic  198 us (46%)
  blocking collectives  84.7 us (19%)
  waiting for transfers between devices  53.9 us (12%)
  matrix products  39 us (9%)
  starting transfers between devices  33.5 us (8%)
  between operations  14.7 us (3%)
  local copies, waits for them, and re-layouts  7.79 us (2%)
    convert_element_type x1, other arithmetic, local(): d_features = (cotangent.astype(jnp.float32) + spread).astype(jnp.bfloat16)  111 us
    psum x1, blocking collectives, local(): lax.psum(lax.psum((d_kern, d_kbias, d_gain, d_shift, d_wup, d_bup, d_wdow...  61.3 us
    psum x1, waiting for transfers between devices, local(): lax.psum((d_kern, d_kbias, d_gain, d_shift, d_wup, d_bup, d_wdown, d_bdow...  47.8 us
    dot_general x6, matrix products, product(): return jnp.einsum(spec, left, right, preferred_element_type=jnp.float32)  39 us
    reduce_sum x1, other arithmetic, layer_back(): chan_mean = jnp.mean(conv_out, axis=-1, keepdims=True)  33 us
    reduce_sum x3, other arithmetic, kernel_grad(): line.append(jnp.sum(slopes_in * window, axis=(0, 1)))  32.6 us
    psum x1, blocking collectives, local(): lax.psum((d_kern, d_kbias, d_gain, d_shift, d_wup, d_bup, d_wdown, d_bdow...  23.4 us
    ppermute x4, starting transfers between devices, extended(): lax.ppermute(tail, axis, [(i, (i + 1) % count) for i in range(count)])  21.8 us
  transfers between devices with their start and end apart: 10, of which 5 were waited for; matrix products, arithmetic and copies ran while one was open for 29% of the time, Pallas kernels for 0%

profile of v1, /device:TPU:1, one launch (start us, length us, event | category | flops | bytes accessed | tf_op | source)
XLA Modules:
  0.0 431.1 jit_solution(16451334733335710789)
XLA Ops:
  7.2 0.0 copy-start
  7.2 0.0 all-reduce.9.cloned.1.call-start
  7.3 0.0 copy-start.3
  7.3 3.1 copy.22
  10.4 0.1 fusion.166
  10.4 2.5 collective-permute-start
  13.0 4.9 %collective-permute-start.1 = (bf16[3,64,128]{2,0,1:T(4,128)(2,1)S(1)}, bf16[3,64,128]{2,0,1:T(4,128)(2,1)S(1)}, u32[]{:S(2)}, u32[]{:S(2)}) collective-permute-start(bf16[3,64,128]{2,0,1:T(4,128)(2,1)S(1)} %get-tuple-element.102), channel_id=1, source_target_pairs={{8,0},{16,8},{24,16},{32,24},{40,32},{48,40},{56,48},{64,56},{72,6... | collective-permute-start | bytes 147464 | tf_op jit(solution)/shard_map/ppermute | solution.py:19
  17.9 0.0 copy-done.6
  18.0 1.1 convert_reduce_fusion.1
  19.1 0.1 collective-permute-done
  19.2 0.1 collective-permute-done.1
  19.2 0.1 pad_maximum_fusion.5
  19.3 2.6 collective-permute-start.2
  21.9 0.0 collective-permute-start.3
  21.9 1.7 collective-permute-done.2
  23.6 2.4 collective-permute-done.3
  26.0 2.9 maximum_select_fusion.1
  29.0 33.0 %fusion.163 = (f32[128,64]{0,1:T(8,128)S(1)}, f32[128,64,128]{2,0,1:T(8,128)S(1)}) fusion(f32[128]{0:T(128)S(1)} %copy-done.11, f32[128]{0:T(128)S(1)} %get-tuple-element.150, bf16[134,70,128]{2,0,1:T(8,128)(2,1)S(1)} %maximum_select_fusion.1, f32[128]{0:T(128)S(1)} %get-tuple-element.151, f32[128]{0:T(128)S(1)} %get-tuple-element.104, ...), kind=kLoop, calls=%fused_computation.403 | loop fusion | flops 155181056 | bytes 107013120 | tf_op jit(solution)/shard_map/reduce_sum | solution.py:87
  62.0 0.0 copy-start.7
  62.0 0.0 copy-start.8
  62.0 0.0 copy-start.9
  62.0 2.7 multiply_reduce_fusion.2
  64.8 0.0 copy-start.4
  64.8 0.0 copy-start.12
  64.8 8.6 %multiply_convert_fusion = (bf16[128,64,512]{2,0,1:T(8,128)(2,1)}, f32[128,64,512]{2,0,1:T(8,128)S(1)}) fusion(f32[512]{0:T(512)S(1)} %copy-done.9, bf16[128,512]{1,0:T(8,128)(2,1)S(1)} %copy-done, f32[128,64,128]{2,0,1:T(8,128)S(1)} %get-tuple-element.94, f32[128]{0:T(128)S(1)} %copy-done.8, f32[128]{0:T(128)S(1)} %copy-done.7, ...), kind=kOutput, calls=%fused_computation.7 | convolution fusion | flops 1104150528 | bytes 29559808 | tf_op jit(solution)/shard_map/rwc,ce->rwe/dot_general | solution.py:36
  73.5 10.9 %convert_reduce_fusion = (f32[512]{0:T(512)S(1)}, bf16[128,64,512]{2,0,1:T(8,128)(2,1)S(1)}) fusion(f32[128,64,512]{2,0,1:T(8,128)S(1)} %get-tuple-element.156, f32[512]{0:T(512)S(1)} %copy-done.9, bf16[512,128]{1,0:T(8,128)(2,1)S(1)} %copy-done.12, f32[128]{0:T(128)S(1)} %copy-done.10, bf16[128,64,128]{2,1,0:T(8,128)(2,1)S(1)} %copy-done.4), kind=kOutput, calls=%fused_computation.8 | convolution fusion | flops 1131412992 | bytes 27398656 | tf_op jit(solution)/shard_map/rwc,ec->rwe/dot_general | solution.py:36
  84.4 4.2 convolution_bitcast_fusion.1
  88.6 4.8 %multiply_reduce_fusion = (f32[128]{0:T(128)S(1)}, f32[128,64]{0,1:T(8,128)S(1)}, f32[128,64]{0,1:T(8,128)S(1)}, f32[128]{0:T(128)S(1)}, f32[128,64,128]{2,0,1:T(8,128)S(1)}) fusion(f32[128,64,128]{2,0,1:T(8,128)S(1)} %get-tuple-element.94, f32[128,64]{0,1:T(8,128)S(1)} %add_rsqrt_fusion, f32[128,64]{0,1:T(8,128)S(1)} %broadcast_multiply_fusion.4, ...), kind=kOutput, calls=%fused_computation.310 | convolution fusion | flops 1083162368 | bytes 17040896 | tf_op jit(solution)/shard_map/rwe,ce->rwc/dot_general | solution.py:36
  93.3 0.0 slice-start
  93.3 13.4 %fusion.102 = (f32[128]{0:T(128)S(1)}, f32[128]{0:T(128)S(1)}, f32[128]{0:T(128)S(1)}, f32[128]{0:T(128)S(1)}, f32[128]{0:T(128)S(1)}, /*index=5*/f32[128]{0:T(1...) fusion(bf16[134,70,128]{2,0,1:T(8,128)(2,1)S(1)} %maximum_selec, ...), kind=kLoop, calls=%fused_computation.208 | loop fusion | flops 63960832 | bytes 50472448 | tf_op jit(solution)/shard_map/reduce_sum | solution.py:72
  106.8 0.0 slice-start.1
  106.8 11.0 %fusion.84 = (f32[128]{0:T(128)S(1)}, f32[128]{0:T(128)S(1)}, f32[128]{0:T(128)S(1)}, f32[128]{0:T(128)S(1)}, f32[128]{0:T(128)S(1)}, /*index=5*/f32[128]{0:T(12...) fusion(f32[128,64,128]{2,0,1:T(8,128)S(1)} %get-tuple-element.9, ...), kind=kLoop, calls=%fused_computation.190 | loop fusion | flops 56620800 | bytes 41952256 | tf_op jit(solution)/shard_map/reduce_sum | solution.py:72
  117.8 0.0 copy-start.5
  117.8 8.2 %fusion.43 = (f32[128]{0:T(128)S(1)}, f32[128]{0:T(128)S(1)}, f32[128]{0:T(128)S(1)}, f32[128]{0:T(128)S(1)}, f32[128]{0:T(128)S(1)}, /*index=5*/f32[128]{0:T(12...) fusion(f32[128,64,128]{2,0,1:T(8,128)S(1)} %get-tuple-element.9, ...), kind=kLoop, calls=%fused_computation.149 | loop fusion | flops 41941248 | bytes 31464448 | tf_op jit(solution)/shard_map/reduce_sum | solution.py:72
  126.2 0.0 copy-start.13
  126.2 4.3 %convolution_bitcast_fusion = f32[512,128]{1,0:T(8,128)} fusion(bf16[128,64,512]{2,0,1:T(8,128)(2,1)S(1)} %bitcast.186, f32[128]{0:T(128)S(1)} %copy-done.10, bf16[128,64,128]{2,1,0:T(8,128)(2,1)S(1)} %copy-done.5), kind=kOutput, calls=%fused_computation.319 | convolution fusion | flops 1076887552 | bytes 10748416 | tf_op jit(solution)/shard_map/rwe,rwc->ec/dot_general | solution.py:36
  130.5 6.2 %fusion.105 = f32[128]{0:T(128)S(1)} fusion(bf16[128,64,512]{2,0,1:T(8,128)(2,1)} %get-tuple-element.155, f32[128]{0:T(128)S(1)} %copy-done.13, bf16[128,64,128]{2,1,0:T(8,128)(2,1)S(1)} %copy-done.5, bf16[512,128]{1,0:T(8,128)(2,1)S(1)} %copy-done.12), kind=kOutput, calls=%fused_computation.211 | convolution fusion | flops 1077936000 | bytes 10617856 | tf_op jit(solution)/shard_map/rwe,ec->rwc/dot_general | solution.py:36
  137.0 23.4 %all-reduce.2 = (f32[7,7,128]{2,1,0:T(8,128)S(1)}, f32[128]{0:T(128)S(1)}, f32[128]{0:T(128)S(1)}, f32[128]{0:T(128)S(1)}, f32[512]{0:T(512)S(1)}, /*index=5*/f32[128]{0:T(128)S(1)}, f32[128]{0:T(128)S(1)}) all-reduce(f32[7,7,128]{2,1,0:T(8,128)S(1)} %constant_dynamic-update-slice_fusion, ...), channel_id=1, replica_groups=mesh['gx'=16,'gy'=8] {'gy'}, use_global_device_ids=true, to_apply=%region_53.54 | all-reduce | flops 7424 | bytes 59392 | tf_op jit(solution)/shard_map/psum | solution.py:143
  160.3 61.3 %all-reduce = (f32[7,7,128]{2,1,0:T(8,128)S(1)}, f32[128]{0:T(128)S(1)}, f32[128]{0:T(128)S(1)}, f32[128]{0:T(128)S(1)}, f32[512]{0:T(512)S(1)}, /*index=5*/f32[128]{0:T(128)S(1)}, f32[128]{0:T(128)S(1)}) all-reduce(f32[7,7,128]{2,1,0:T(8,128)S(1)} %get-tuple-element.83, ...), channel_id=1, replica_groups=mesh['gx'=16,'gy'=8] {'gx'}, use_global_device_ids=true, to_apply=%region_54.55 | all-reduce | flops 7424 | bytes 59392 | tf_op jit(solution)/shard_map/psum | solution.py:142
  221.7 0.6 broadcast_multiply_fusion.5
  222.3 0.6 broadcast_multiply_fusion.6
  222.8 0.5 broadcast_multiply_fusion.10
  223.4 0.5 broadcast_multiply_fusion.11
  223.9 0.5 broadcast_multiply_fusion.7
  224.4 0.0 collective-permute-start.4
  224.4 4.8 %collective-permute-start.5 = (f32[3,64,128]{2,0,1:T(4,128)S(1)}, f32[3,64,128]{2,0,1:T(4,128)S(1)}, u32[]{:S(2)}, u32[]{:S(2)}) collective-permute-start(f32[3,64,128]{2,0,1:T(4,128)S(1)} %get-tuple-element.98), channel_id=1, source_target_pairs={{8,0},{16,8},{24,16},{32,24},{40,32},{48,40},{56,48},{64,56},{72,6... | collective-permute-start | bytes 294920 | tf_op jit(solution)/shard_map/ppermute | solution.py:19
  229.2 0.5 broadcast_multiply_fusion.8
  229.7 0.0 all-reduce.9.cloned.1.call-update
  229.7 0.0 all-reduce.7.cloned.1.call-start
  229.8 1.8 collective-permute-done.4
  231.6 0.0 collective-permute-done.5
  231.6 1.1 pad_maximum_fusion.2
  232.6 16.7 %collective-permute-start.6 = (f32[134,3,128]{2,0,1:T(8,128)S(1)}, f32[134,3,128]{2,0,1:T(8,128)S(1)}, u32[]{:S(2)}, u32[]{:S(2)}) collective-permute-start(f32[134,3,128]{2,0,1:T(8,128)S(1)} %get-tuple-element.95), channel_id=1, source_target_pairs={{0,1},{1,2},{2,3},{3,4},{4,5},{5,6},{6,7},{7,0},{8,9},{9,10},{10,1... | collective-permute-start | bytes 617480 | tf_op jit(solution)/shard_map/ppermute | solution.py:17
  249.3 1.9 collective-permute-start.7
  251.2 0.5 broadcast_multiply_fusion.9
  251.7 47.8 %all-reduce.9.cloned.1.call-done = (f32[128,512]{1,0:T(8,128)}, f32[512,128]{1,0:T(8,128)}) async-done(((f32[128,512]{1,0:T(8,128)}, f32[512,128]{1,0:T(8,128)}), (f32[128,512]{1,0:T(8,128)}, f32[512,128]{1,0:T(8,128)})) %all-reduce.9.cloned.1.call-update) | async-done | bytes 524304 | tf_op jit(solution)/shard_map/psum | solution.py:143
  299.5 0.0 all-reduce.7.cloned.1.call-update
  299.6 0.0 collective-permute-done.6
  299.6 0.0 collective-permute-done.7
  299.6 5.5 %maximum_select_fusion = f32[134,70,128]{2,0,1:T(8,128)} fusion(f32[134,3,128]{2,0,1:T(8,128)S(1)} %collective-permute-done.7, f32[3,64,128]{2,0,1:T(4,128)S(1)} %collective-permute-done.5, f32[128,64,128]{2,0,1:T(8,128)} %copy-done.2, f32[3,64,128]{2,0,1:T(4,128)S(1)} %collective-permute-done.4, f32[134,3,128]{2,0,1:T(8,128)S(1)} %collective-permute-done.6, ...), kind=kLoop, calls=%fused_computation.111 | loop fusion | flops 6003200 | bytes 9605190 | tf_op jit(solution)/shard_map/jit(_where)/select_n | solution.py:83
  305.1 111.4 %fusion.104 = bf16[128,64,128]{2,0,1:T(8,128)(2,1)} fusion(f32[134,70,128]{2,0,1:T(8,128)} %maximum_select_fusion, f32[128]{0:T(128)S(1)} %get-tuple-element.150, f32[128]{0:T(128)S(1)} %get-tuple-element.151, f32[128]{0:T(128)S(1)} %get-tuple-element.104, f32[128]{0:T(128)S(1)} %get-tuple-element.105, f32[128]{0:T(128)S(1)} %get-tuple-element.106, ...), kind=kLoop, calls=%fused_computation.210 | loop fusion | flops 104857600 | bytes 209740288 | tf_op jit(solution)/shard_map/convert_element_type | solution.py:140
  416.5 4.3 copy.27
  420.7 1.7 broadcast_multiply_fusion
  422.4 1.7 broadcast_multiply_fusion.1
  (44 shorter events, 0.4 us)
Async XLA Ops:
  7.2 57.6 %copy-start = (bf16[128,512]{1,0:T(8,128)(2,1)S(1)}, bf16[128,512]{1,0:T(8,128)(2,1)}, u32[]{:S(2)}) copy-start(bf16[128,512]{1,0:T(8,128)(2,1)} %param.17) | copy-start | bytes 393220
  7.2 10.7 %copy-start.6 = (f32[7,7,128]{2,1,0:T(8,128)S(1)}, f32[7,7,128]{2,1,0:T(8,128)}, u32[]{:S(2)}) copy-start(f32[7,7,128]{2,1,0:T(8,128)} %param.13) | copy-start | bytes 75268
  7.2 10.7 %copy-start.10 = (f32[128]{0:T(128)S(1)}, f32[128]{0:T(128)}, u32[]{:S(2)}) copy-start(f32[128]{0:T(128)} %param.21) | copy-start | bytes 1540
  7.2 292.3 %all-reduce.9.cloned.1.call-start = ((), (), s32[]{:S(2)}) async-start(), calls=%async_computation.1 | async-start | bytes 1048576 | tf_op jit(solution)/shard_map/psum | solution.py:143
  7.3 10.7 %copy-start.3 = (bf16[128,64,128]{2,1,0:T(8,128)(2,1)S(1)}, bf16[128,64,128]{2,1,0:T(8,128)(2,1)}, u32[]{:S(2)}) copy-start(bf16[128,64,128]{2,1,0:T(8,128)(2,1)} %param.12) | copy-start | bytes 6291460
  10.4 8.8 %collective-permute-start = (bf16[3,64,128]{2,0,1:T(4,128)(2,1)S(1)}, bf16[3,64,128]{2,0,1:T(4,128)(2,1)S(1)}, u32[]{:S(2)}, u32[]{:S(2)}) collective-permute-start(bf16[3,64,128]{2,0,1:T(4,128)(2,1)S(1)} %get-tuple-element.101), channel_id=1, source_target_pairs={{0,8},{8,16},{16,24},{24,32},{32,40},{40,48},{48,56},{56,64},{64,7... | collective-permute-start | bytes 147464 | tf_op jit(solution)/shard_map/ppermute | solution.py:17
  13.0 6.3 %collective-permute-start.1 = (bf16[3,64,128]{2,0,1:T(4,128)(2,1)S(1)}, bf16[3,64,128]{2,0,1:T(4,128)(2,1)S(1)}, u32[]{:S(2)}, u32[]{:S(2)}) collective-permute-start(bf16[3,64,128]{2,0,1:T(4,128)(2,1)S(1)} %get-tuple-element.102), channel_id=1, source_target_pairs={{8,0},{16,8},{24,16},{32,24},{40,32},{48,40},{56,48},{64,56},{72,6... | collective-permute-start | bytes 147464 | tf_op jit(solution)/shard_map/ppermute | solution.py:19
  19.1 9.9 %copy-start.11 = (f32[128]{0:T(128)S(1)}, f32[128]{0:T(128)}, u32[]{:S(2)}) copy-start(f32[128]{0:T(128)} %param.14) | copy-start | bytes 1540
  19.3 4.3 %collective-permute-start.2 = (bf16[134,3,128]{2,0,1:T(8,128)(2,1)S(1)}, bf16[134,3,128]{2,0,1:T(8,128)(2,1)S(1)}, u32[]{:S(2)}, u32[]{:S(2)}) collective-permute-start(bf16[134,3,128]{2,0,1:T(8,128)(2,1)S(1)} %get-tuple-element.99), channel_id=1, source_target_pairs={{0,1},{1,2},{2,3},{3,4},{4,5},{5,6},{6,7},{7,0},{8,9},{9,10},{10,1... | collective-permute-start | bytes 308744 | tf_op jit(solution)/shard_map/ppermute | solution.py:17
  21.9 4.1 collective-permute-start.3
  62.0 2.8 copy-start.7
  62.0 2.8 copy-start.8
  62.0 2.8 copy-start.9
  64.8 8.7 %copy-start.4 = (bf16[128,64,128]{2,1,0:T(8,128)(2,1)S(1)}, bf16[128,64,128]{2,1,0:T(8,128)(2,1)}, u32[]{:S(2)}) copy-start(bf16[128,64,128]{2,1,0:T(8,128)(2,1)} %param.12) | copy-start | bytes 6291460
  64.8 8.6 %copy-start.12 = (bf16[512,128]{1,0:T(8,128)(2,1)S(1)}, bf16[512,128]{1,0:T(8,128)(2,1)}, u32[]{:S(2)}) copy-start(bf16[512,128]{1,0:T(8,128)(2,1)} %param.19) | copy-start | bytes 393220
  93.3 32.8 %slice-start = ((s8[8388608]{0:T(1024)(128)(4,1)}), s8[4194304]{0:T(1024)(128)(4,1)S(1)}, s32[]{:S(2)}) async-start(s8[8388608]{0:T(1024)(128)(4,1)} %bitcast.185), calls=%async_computation.2 | async-start | bytes 8388608
  106.7 19.3 %copy-start.2 = (f32[128,64,128]{2,0,1:T(8,128)}, f32[128,64,128]{2,0,1:T(8,128)S(1)}, u32[]{:S(2)}) copy-start(f32[128,64,128]{2,0,1:T(8,128)S(1)} %get-tuple-element.92) | copy-start | bytes 12582916
  106.8 19.4 %slice-start.1 = ((s8[8388608]{0:T(1024)(128)(4,1)}), s8[4194304]{0:T(1024)(128)(4,1)S(1)}, s32[]{:S(2)}) async-start(s8[8388608]{0:T(1024)(128)(4,1)} %bitcast.185), calls=%async_computation.3 | async-start | bytes 8388608
  117.8 8.3 %copy-start.5 = (bf16[128,64,128]{2,1,0:T(8,128)(2,1)S(1)}, bf16[128,64,128]{2,1,0:T(8,128)(2,1)}, u32[]{:S(2)}) copy-start(bf16[128,64,128]{2,1,0:T(8,128)(2,1)} %param.12) | copy-start | bytes 6291460
  126.2 4.4 %copy-start.13 = (f32[128]{0:T(128)S(1)}, f32[128]{0:T(128)}, u32[]{:S(2)}) copy-start(f32[128]{0:T(128)} %param.20) | copy-start | bytes 1540
  224.4 7.2 %collective-permute-start.4 = (f32[3,64,128]{2,0,1:T(4,128)S(1)}, f32[3,64,128]{2,0,1:T(4,128)S(1)}, u32[]{:S(2)}, u32[]{:S(2)}) collective-permute-start(f32[3,64,128]{2,0,1:T(4,128)S(1)} %get-tuple-element.97), channel_id=1, source_target_pairs={{0,8},{8,16},{16,24},{24,32},{32,40},{40,48},{48,56},{56,64},{64,7... | collective-permute-start | bytes 294920 | tf_op jit(solution)/shard_map/ppermute | solution.py:17
  224.4 7.2 %collective-permute-start.5 = (f32[3,64,128]{2,0,1:T(4,128)S(1)}, f32[3,64,128]{2,0,1:T(4,128)S(1)}, u32[]{:S(2)}, u32[]{:S(2)}) collective-permute-start(f32[3,64,128]{2,0,1:T(4,128)S(1)} %get-tuple-element.98), channel_id=1, source_target_pairs={{8,0},{16,8},{24,16},{32,24},{40,32},{48,40},{56,48},{64,56},{72,6... | collective-permute-start | bytes 294920 | tf_op jit(solution)/shard_map/ppermute | solution.py:19
  229.7 191.0 %all-reduce.7.cloned.1.call-start = ((), (), s32[]{:S(2)}) async-start(), calls=%async_computation | async-start | bytes 1048576 | tf_op jit(solution)/shard_map/psum | solution.py:142
  232.6 66.9 %collective-permute-start.6 = (f32[134,3,128]{2,0,1:T(8,128)S(1)}, f32[134,3,128]{2,0,1:T(8,128)S(1)}, u32[]{:S(2)}, u32[]{:S(2)}) collective-permute-start(f32[134,3,128]{2,0,1:T(8,128)S(1)} %get-tuple-element.95), channel_id=1, source_target_pairs={{0,1},{1,2},{2,3},{3,4},{4,5},{5,6},{6,7},{7,0},{8,9},{9,10},{10,1... | collective-permute-start | bytes 617480 | tf_op jit(solution)/shard_map/ppermute | solution.py:17
  249.3 50.3 %collective-permute-start.7 = (f32[134,3,128]{2,0,1:T(8,128)S(1)}, f32[134,3,128]{2,0,1:T(8,128)S(1)}, u32[]{:S(2)}, u32[]{:S(2)}) collective-permute-start(f32[134,3,128]{2,0,1:T(8,128)S(1)} %get-tuple-element.96), channel_id=1, source_target_pairs={{1,0},{2,1},{3,2},{4,3},{5,4},{6,5},{7,6},{0,7},{9,8},{10,9},{11,1... | collective-permute-start | bytes 617480 | tf_op jit(solution)/shard_map/ppermute | solution.py:19
  305.1 119.0 %copy-start.1 = (bf16[128,512]{1,0:T(8,128)(2,1)S(1)}, bf16[128,512]{1,0:T(8,128)(2,1)}, u32[]{:S(2)}) copy-start(bf16[128,512]{1,0:T(8,128)(2,1)} %param.17) | copy-start | bytes 393220
Sparse Core Ops, SparseCore 0:
  229.8 69.6 all-reduce.8
  302.8 85.7 all-reduce.6
